TPU v7x, 32 devices: a whole 2x2x4 slice. The times are simulated.
32 devices in a mesh: wide: 8 (over y, x, core), narrow: 4 (over z).
Axes of the slice: x: 2, y: 2, z: 4, core: 2. Of those that a mesh axis runs over, the one named last changes fastest.
Arguments:
- row_vectors: bfloat16 [8192, 2048], P('wide'), may hold values from -0.59765625 to 1.3984375
- col_vectors: bfloat16 [2048, 2048], P('narrow', 'wide'), may hold values from -0.59765625 to 1.3984375
- primal_matrix: bfloat16 [2048, 2048], P('wide'), may hold values from -1 to 3, as said below
- dual_inverse: bfloat16 [2048, 2048], P('wide'), may hold values from -1 to 3, as said below
Outputs:
- factored: float32 [8192, 2048], P('wide', 'narrow')
Inputs may be any that keep to these rules, and one draw needn't show every extreme that they name: `primal_matrix`: symmetric positive definite. `dual_inverse`: symmetric positive definite.
All inputs are finite; a program needn't handle non-finite values.
Results may differ from a plain program's by a relative error of at most 0.0027.
Values may be sent and summed in bfloat16 or wider, within the bound.
No kernel may reach another device: no remote copies, remote signals or barrier semaphores. Data moves between devices by JAX's collectives and lax.ppermute only.
A program may use at most 64 MiB of HBM per device.

v0:
```python
import jax
import jax.numpy as jnp
from jax import lax
from jax.sharding import PartitionSpec as P


def spread(value, axis, source):
    kept = jnp.where(lax.axis_index(axis) == source, value, 0).astype(value.dtype)
    return lax.psum(kept, axis)


def per_device(row_vectors, col_vectors, primal_matrix, dual_inverse):
    wide_count = lax.axis_size("wide")
    wide_index = lax.axis_index("wide")
    narrow_index = lax.axis_index("narrow")
    cone_order = primal_matrix.shape[1]
    panel_width = col_vectors.shape[0]
    panel_share = panel_width // wide_count
    gram_scale = 16.0 / (cone_order * cone_order)
    column_set = lax.all_gather(col_vectors, "wide", axis=1, tiled=True)
    local_panel = lax.dynamic_slice_in_dim(column_set, wide_index * panel_share, panel_share, 0)
    panel_set = spread(local_panel, "narrow", 0)
    prod_primal = jnp.dot(primal_matrix, column_set.T, preferred_element_type=jnp.float32).astype(
        jnp.bfloat16
    )
    prod_dual = jnp.dot(dual_inverse, column_set.T, preferred_element_type=jnp.float32).astype(
        jnp.bfloat16
    )
    pieces = (
        lax.all_gather(prod_primal, "wide", axis=0, tiled=True),
        lax.all_gather(prod_dual, "wide", axis=0, tiled=True),
    )
    row_slice = row_vectors
    panel_slice = panel_set
    gram_primal = jnp.dot(row_slice, pieces[0], preferred_element_type=jnp.float32)
    gram_dual = jnp.dot(row_slice, pieces[1], preferred_element_type=jnp.float32)
    tile_primal = jnp.dot(panel_slice, pieces[0], preferred_element_type=jnp.float32)
    tile_dual = jnp.dot(panel_slice, pieces[1], preferred_element_type=jnp.float32)
    slab = gram_primal * gram_dual * gram_scale
    panel_tile = tile_primal * tile_dual * gram_scale
    gram = lax.all_gather(panel_tile, "wide", axis=0, tiled=True)
    panel_primal, panel_dual = (spread(prod_primal, "narrow", 0), spread(prod_dual, "narrow", 0))
    pieces = (
        lax.all_gather(panel_primal, "wide", axis=0, tiled=True),
        lax.all_gather(panel_dual, "wide", axis=0, tiled=True),
    )
    row_slice = row_vectors
    panel_slice = panel_set
    first_primal = jnp.dot(row_slice, pieces[0], preferred_element_type=jnp.float32)
    first_dual = jnp.dot(row_slice, pieces[1], preferred_element_type=jnp.float32)
    diag_primal = jnp.dot(panel_slice, pieces[0], preferred_element_type=jnp.float32)
    diag_dual = jnp.dot(panel_slice, pieces[1], preferred_element_type=jnp.float32)
    slab_first = first_primal * first_dual * gram_scale
    diag_share = diag_primal * diag_dual * gram_scale
    diag_block = lax.all_gather(diag_share, "wide", axis=0, tiled=True)
    factor = jnp.linalg.cholesky(diag_block)
    panel_cols = jax.scipy.linalg.solve_triangular(factor, slab_first.T, lower=True).T
    solved = jax.scipy.linalg.solve_triangular(factor, gram, lower=True)
    trailing = slab - jnp.dot(panel_cols, solved, precision=lax.Precision.HIGHEST)
    return jnp.where(narrow_index == 0, panel_cols, trailing)


def solution(mesh):
    placed = (P("wide", None), P("narrow", "wide"), P("wide", None), P("wide", None))
    return jax.shard_map(
        per_device, mesh=mesh, in_specs=placed, out_specs=P("wide", "narrow"), check_vma=False
    )
```

profile of v0, /device:TPU:0, one launch (start us, length us, event | category | flops | bytes accessed | tf_op | source)
XLA Modules:
  0.0 404.9 jit_solution(14323535029194417202)
XLA Ops:
  6.5 0.7 all-gather.8.cloned.1.call-update
  7.3 32.8 %all-gather.8.cloned.1.call-done = bf16[512,2048]{1,0:T(8,128)(2,1)} async-done(((bf16[512,256]{1,0:T(8,128)(2,1)}), bf16[512,2048]{1,0:T(8,128)(2,1)}) %all-gather.8.cloned.1.call-update) | async-done | bytes 2097168 | tf_op jit(solution)/shard_map/all_gather | solution.py:20
  40.1 3.3 broadcast_select_fusion.1
  43.4 1.6 broadcast_select_fusion
  45.0 0.7 dynamic-slice_select_fusion
  45.8 44.0 %all-reduce.4.cloned.1.call-done = (bf16[256,512]{1,0:T(8,128)(2,1)}, bf16[256,512]{1,0:T(8,128)(2,1)}, bf16[64,2048]{1,0:T(8,128)(2,1)}) async-done(((bf16[256,512]{1,0:T(8,128)(2,1)}, bf16[256,512]{1,0:T(8,128)(2,1)}, bf16[64,2048]{1,0:T(8,128)(2,1)}), (bf16[256,512]{1,0:T(8,128)(2,1)}, bf16[256,512]{1,0:T(8,128)(2,1)}, bf16[64,2048]{1,0:T(8,128)(2,1)})) %all-reduce.4.cloned.1.call-update) | async-done | bytes 786448 | tf_op jit(solution)/shard_map/psum | solution.py:9
  91.6 27.0 %all-gather.10.cloned.1.call-done = bf16[2048,512]{1,0:T(8,128)(2,1)} async-done(((bf16[256,512]{1,0:T(8,128)(2,1)}), bf16[2048,512]{1,0:T(8,128)(2,1)}) %all-gather.10.cloned.1.call-update) | async-done | bytes 2097168 | tf_op jit(solution)/shard_map/all_gather | solution.py:44
  118.7 2.2 fusion.65
  120.9 27.4 %all-gather.12.cloned.1.call-done = bf16[2048,512]{1,0:T(8,128)(2,1)} async-done(((bf16[256,512]{1,0:T(8,128)(2,1)}), bf16[2048,512]{1,0:T(8,128)(2,1)}) %all-gather.12.cloned.1.call-update) | async-done | bytes 2097168 | tf_op jit(solution)/shard_map/all_gather | solution.py:45
  148.2 2.7 fusion.12
  151.2 26.6 %all-gather.16.cloned.1.call-done = bf16[2048,512]{1,0:T(8,128)(2,1)} async-done(((bf16[256,512]{1,0:T(8,128)(2,1)}), bf16[2048,512]{1,0:T(8,128)(2,1)}) %all-gather.16.cloned.1.call-update) | async-done | bytes 2097168 | tf_op jit(solution)/shard_map/all_gather | solution.py:30
  177.8 2.2 fusion.68
  180.0 27.3 %all-gather.18.cloned.1.call-done = bf16[2048,512]{1,0:T(8,128)(2,1)} async-done(((bf16[256,512]{1,0:T(8,128)(2,1)}), bf16[2048,512]{1,0:T(8,128)(2,1)}) %all-gather.18.cloned.1.call-update) | async-done | bytes 2097168 | tf_op jit(solution)/shard_map/all_gather | solution.py:31
  207.3 2.7 fusion.11
  210.1 6.0 %fusion.67 = f32[512,1024]{1,0:T(8,128)} fusion(bf16[2048,512]{1,0:T(8,128)(2,1)S(1)} %copy-done.8, bf16[1024,2048]{1,0:T(8,128)(2,1)} %param.4), kind=kOutput, calls=%fused_computation.112 | convolution fusion | flops 2147483648 | bytes 8388608 | tf_op jit(solution)/shard_map/dot_general | solution.py:35
  216.1 2.4 fusion.66
  218.6 3.7 multiply_multiply_fusion
  222.3 10.4 %all-gather.14.cloned.1.call-done = f32[512,512]{1,0:T(8,128)} async-done(((f32[64,512]{1,0:T(8,128)}), f32[512,512]{1,0:T(8,128)}) %all-gather.14.cloned.1.call-update) | async-done | bytes 1048592 | tf_op jit(solution)/shard_map/all_gather | solution.py:55
  232.6 1.6 copy.12
  234.5 1.0 copy-done.3
  235.5 11.9 %cholesky.104 = f32[128,128]{1,0:T(8,128)S(1)} custom-call(f32[128,128]{1,0:T(8,128)S(1)} %cholesky.266), custom_call_target="Cholesky" | custom-call | tf_op jit(solution)/shard_map/jit(cholesky)/cholesky | solution.py:56
  247.6 9.8 %custom-call.34 = f32[1,128,128]{1,2,0:T(8,128)S(1)} custom-call(f32[1,128,128]{2,1,0:T(8,128)S(1)} %get-tuple-element.35), custom_call_target="InvertDiagBlocksLowerTriangular" | custom-call | tf_op jit(solution)/shard_map/jit(cholesky)/cholesky | solution.py:56
  257.4 1.2 constant_dynamic-update-slice_fusion.3
  258.6 1.3 convolution_subtract_fusion.5
  259.9 11.7 %cholesky.217 = f32[128,128]{1,0:T(8,128)S(1)} custom-call(f32[128,128]{1,0:T(8,128)S(1)} %cholesky.270), custom_call_target="Cholesky" | custom-call | tf_op jit(solution)/shard_map/jit(cholesky)/cholesky | solution.py:56
  271.7 9.8 %custom-call.35 = f32[1,128,128]{1,2,0:T(8,128)S(1)} custom-call(f32[1,128,128]{2,1,0:T(8,128)S(1)} %get-tuple-element.32), custom_call_target="InvertDiagBlocksLowerTriangular" | custom-call | tf_op jit(solution)/shard_map/jit(cholesky)/cholesky | solution.py:56
  281.8 1.3 convolution_subtract_fusion.6
  283.1 12.1 %cholesky.238 = f32[128,128]{1,0:T(8,128)S(1)} custom-call(f32[128,128]{1,0:T(8,128)S(1)} %cholesky.275), custom_call_target="Cholesky" | custom-call | tf_op jit(solution)/shard_map/jit(cholesky)/cholesky | solution.py:56
  295.2 9.8 %custom-call.36 = f32[1,128,128]{1,2,0:T(8,128)S(1)} custom-call(f32[1,128,128]{2,1,0:T(8,128)S(1)} %get-tuple-element.29), custom_call_target="InvertDiagBlocksLowerTriangular" | custom-call | tf_op jit(solution)/shard_map/jit(cholesky)/cholesky | solution.py:56
  305.2 1.2 convolution_subtract_fusion.7
  306.5 11.7 %cholesky.255 = f32[128,128]{1,0:T(8,128)S(1)} custom-call(f32[128,128]{1,0:T(8,128)S(1)} %convolution_subtract_fusion.7), custom_call_target="Cholesky" | custom-call | tf_op jit(solution)/shard_map/jit(cholesky)/cholesky | solution.py:56
  318.9 0.7 compare_reduce_fusion
  323.1 10.8 %while.1 = (s32[]{:T(128)}, f32[512,512]{1,0:T(8,128)S(1)}, s32[4,2]{0,1:T(2,128)S(1)}, f32[4,128,128]{2,1,0:T(8,128)}, s32[]{:T(128)}) while((s32[]{:T(128)}, f32[512,512]{1,0:T(8,128)S(1)}, s32[4,2]{0,1:T(2,128)S(1)}, f32[4,128,128]{2,1,0:T(8,128)}, s32[]{:T(128)}) %tuple.29), condition=%wide.while_cond, body=%wide.while_body.sunk | while | flops 2 | bytes 132205 | solution.py:57
  323.8 2.0 bitcast_dynamic-update-slice_fusion.2
  326.5 2.0 bitcast_dynamic-update-slice_fusion.2
  329.2 2.0 bitcast_dynamic-update-slice_fusion.2
  331.9 2.0 bitcast_dynamic-update-slice_fusion.2
  333.9 40.3 %custom-call.37 = f32[4,128,128]{1,2,0:T(8,128)S(1)} custom-call(f32[4,128,128]{2,1,0:T(8,128)} %get-tuple-element.12), custom_call_target="InvertDiagBlocksLowerTriangular" | custom-call | tf_op jit(solution)/shard_map/jit(_solve_triangular)/triangular_solve | solution.py:57
  374.2 1.8 fusion.29
  376.1 1.6 convolution_subtract_fusion.1
  378.3 0.7 convolution_subtract_fusion
  379.7 1.1 fusion.7
  380.8 1.4 fusion.56
  382.3 1.5 fusion.34
  383.7 1.3 convolution_subtract_fusion.3
  387.5 3.6 fusion.10
  391.1 3.8 fusion
  395.0 2.9 copy.14
  (83 shorter events, 10.9 us)
Async XLA Ops:
  6.5 33.5 %copy-start = (bf16[256,2048]{1,0:T(8,128)(2,1)S(1)}, bf16[256,2048]{1,0:T(8,128)(2,1)}, u32[]{:S(2)}) copy-start(bf16[256,2048]{1,0:T(8,128)(2,1)} %param.6) | copy-start | bytes 3145732
  6.5 36.8 %copy-start.16 = (bf16[256,2048]{1,0:T(8,128)(2,1)S(1)}, bf16[256,2048]{1,0:T(8,128)(2,1)}, u32[]{:S(2)}) copy-start(bf16[256,2048]{1,0:T(8,128)(2,1)} %param.7) | copy-start | bytes 3145732
  6.5 33.5 %all-gather.8.cloned.1.call-start = ((), (), s32[]{:S(2)}) async-start(), calls=%async_computation | async-start | bytes 2359296 | tf_op jit(solution)/shard_map/all_gather | solution.py:20
  7.3 82.6 %all-reduce.4.cloned.1.call-start = ((), (), s32[]{:S(2)}) async-start(), calls=%async_computation.7 | async-start | bytes 1572864 | tf_op jit(solution)/shard_map/psum | solution.py:9
  40.1 3.3 copy-start.13
  45.7 73.0 %all-gather.10.cloned.1.call-start = ((), (), s32[]{:S(2)}) async-start(), calls=%async_computation.1 | async-start | bytes 2359296 | tf_op jit(solution)/shard_map/all_gather | solution.py:44
  89.8 58.4 %copy-start.1 = (bf16[64,2048]{1,0:T(8,128)(2,1)S(1)}, bf16[64,2048]{1,0:T(8,128)(2,1)}, u32[]{:S(2)}) copy-start(bf16[64,2048]{1,0:T(8,128)(2,1)} %get-tuple-element.23) | copy-start | bytes 786436
  89.9 58.4 %all-gather.12.cloned.1.call-start = ((), (), s32[]{:S(2)}) async-start(), calls=%async_computation.2 | async-start | bytes 2359296 | tf_op jit(solution)/shard_map/all_gather | solution.py:45
  90.4 87.3 %all-gather.16.cloned.1.call-start = ((), (), s32[]{:S(2)}) async-start(), calls=%async_computation.4 | async-start | bytes 2359296 | tf_op jit(solution)/shard_map/all_gather | solution.py:30
  91.0 116.3 %all-gather.18.cloned.1.call-start = ((), (), s32[]{:S(2)}) async-start(), calls=%async_computation.5 | async-start | bytes 2359296 | tf_op jit(solution)/shard_map/all_gather | solution.py:31
  91.6 141.0 %all-gather.14.cloned.1.call-start = ((), (), s32[]{:S(2)}) async-start(), calls=%async_computation.3 | async-start | bytes 1179648 | tf_op jit(solution)/shard_map/all_gather | solution.py:55
  151.0 231.3 %all-gather.20.cloned.1.call-start = ((), (), s32[]{:S(2)}) async-start(), calls=%async_computation.6 | async-start | bytes 1179648 | tf_op jit(solution)/shard_map/all_gather | solution.py:41
  177.8 32.3 %copy-start.8 = (bf16[2048,512]{1,0:T(8,128)(2,1)S(1)}, bf16[2048,512]{1,0:T(8,128)(2,1)}, u32[]{:S(2)}) copy-start(bf16[2048,512]{1,0:T(8,128)(2,1)} %all-gather.16.cloned.1.call-done) | copy-start | bytes 6291460
  210.1 6.0 %copy-start.7 = (bf16[2048,512]{1,0:T(8,128)(2,1)S(1)}, bf16[2048,512]{1,0:T(8,128)(2,1)}, u32[]{:S(2)}) copy-start(bf16[2048,512]{1,0:T(8,128)(2,1)} %all-gather.10.cloned.1.call-done) | copy-start | bytes 6291460
  210.1 6.0 %copy-start.14 = (bf16[1024,2048]{1,0:T(8,128)(2,1)S(1)}, bf16[1024,2048]{1,0:T(8,128)(2,1)}, u32[]{:S(2)}) copy-start(bf16[1024,2048]{1,0:T(8,128)(2,1)} %param.4) | copy-start | bytes 12582916
  216.1 2.4 copy-start.5
  232.6 1.7 copy-start.2
  234.5 1.0 copy-start.3
  374.2 4.1 %copy-start.6 = (f32[512,1024]{1,0:T(8,128)S(1)}, f32[512,1024]{1,0:T(8,128)}, u32[]{:S(2)}) copy-start(f32[512,1024]{1,0:T(8,128)} %multiply_multiply_fusion) | copy-start | bytes 6291460
  379.7 1.1 copy-start.9
  382.3 3.2 copy-start.11
  385.1 2.4 copy-start.10
  385.1 2.4 copy-start.12
  386.4 4.7 %copy-start.17 = (f32[512,1024]{1,0:T(8,128)S(1)}, f32[512,1024]{1,0:T(8,128)}, u32[]{:S(2)}) copy-start(f32[512,1024]{1,0:T(8,128)} %fusion.67) | copy-start | bytes 6291460
  387.5 3.7 copy-start.4
  387.5 3.7 copy-start.15
Sparse Core Ops, SparseCore 0:
  9.2 30.8 all-gather.7
  45.9 43.9 all-reduce.3
  91.7 26.9 all-gather.9
  120.4 27.7 all-gather.11
  150.0 27.7 all-gather.15
  179.5 27.7 all-gather.17
  209.2 23.3 all-gather.13
  234.5 23.5 all-gather.19
where the time goes:
time: 408 us; the launch traced here: 405 us
  waiting for transfers between devices  198 us (49%)
  other arithmetic  120 us (29%)
  matrix products  52.8 us (13%)
  between operations  16.8 us (4%)
  local copies, waits for them, and re-layouts  16.5 us (4%)
    another operation x14, other arithmetic, per_device(): factor = jnp.linalg.cholesky(diag_block)  79.1 us
    psum x1, waiting for transfers between devices, spread(): return lax.psum(kept, axis)  44 us
    another operation x3, other arithmetic, per_device(): jax.scipy.linalg.solve_triangular(factor, slab_first.T, lower=True)  40.4 us
    all_gather x1, waiting for transfers between devices, per_device(): column_set = lax.all_gather(col_vectors, 'wide', axis=1, tiled=True)  32.8 us
    all_gather x1, waiting for transfers between devices, per_device(): lax.all_gather(panel_dual, 'wide', axis=0, tiled=True)  27.4 us
    all_gather x1, waiting for transfers between devices, per_device(): lax.all_gather(prod_dual, 'wide', axis=0, tiled=True)  27.3 us
    all_gather x1, waiting for transfers between devices, per_device(): lax.all_gather(panel_primal, 'wide', axis=0, tiled=True)  27 us
    all_gather x1, waiting for transfers between devices, per_device(): lax.all_gather(prod_primal, 'wide', axis=0, tiled=True)  26.6 us
  transfers between devices with their start and end apart: 8, of which 7 were waited for; matrix products, arithmetic and copies ran while one was open for 41% of the time, Pallas kernels for 0%

commit v1 on v0

--- a/solution.py
+++ b/solution.py
@@ -6,7 +6,10 @@
 
 def spread(value, axis, source):
     kept = jnp.where(lax.axis_index(axis) == source, value, 0).astype(value.dtype)
-    return lax.psum(kept, axis)
+    handle_the_lots_all = lambda chip_axis, array_here: jnp.sum(
+        lax.all_gather(array_here, axis_name=chip_axis), axis=0
+    )
+    return handle_the_lots_all(axis, kept)
 
 
 def per_device(row_vectors, col_vectors, primal_matrix, dual_inverse):

time: 408 us -> 448 us (1.098)
  waiting for transfers between devices: 198 us -> 231 us
  other arithmetic: 120 us -> 126 us
    all_gather x0 -> x3, waiting for transfers between devices: none -> 76.2 us  [spread(): lax.all_gather(array_here, axis_name=chip_axis)]
    psum x1 -> x0, waiting for transfers between devices: 44 us -> none  [spread(): return lax.psum(kept, axis)]
    reduce_sum x0 -> x3, other arithmetic: none -> 5.7 us  [spread(): jnp.sum(lax.all_gather(array_here, axis_name=chip_axis), axis=0)]
  transfers between devices with their start and end apart: 8 -> 10, of which waited for: 7 -> 9; matrix products, arithmetic and copies ran while one was open for 41% -> 40% of each run, Pallas kernels for 0% -> 0%
where the time goes in v1:
time: 448 us; the launch traced here: 444 us
  waiting for transfers between devices  231 us (52%)
  other arithmetic  126 us (28%)
  matrix products  53.8 us (12%)
  between operations  16.7 us (4%)
  local copies, waits for them, and re-layouts  16.3 us (4%)
    another operation x14, other arithmetic, per_device(): factor = jnp.linalg.cholesky(diag_block)  79 us
    all_gather x3, waiting for transfers between devices, spread(): lax.all_gather(array_here, axis_name=chip_axis)  76.2 us
    another operation x3, other arithmetic, per_device(): jax.scipy.linalg.solve_triangular(factor, slab_first.T, lower=True)  40.4 us
    all_gather x1, waiting for transfers between devices, per_device(): column_set = lax.all_gather(col_vectors, 'wide', axis=1, tiled=True)  32.8 us
    all_gather x1, waiting for transfers between devices, per_device(): lax.all_gather(panel_primal, 'wide', axis=0, tiled=True)  27.5 us
    all_gather x1, waiting for transfers between devices, per_device(): lax.all_gather(panel_dual, 'wide', axis=0, tiled=True)  27.5 us
    all_gather x1, waiting for transfers between devices, per_device(): lax.all_gather(prod_dual, 'wide', axis=0, tiled=True)  27.5 us
    all_gather x1, waiting for transfers between devices, per_device(): lax.all_gather(prod_primal, 'wide', axis=0, tiled=True)  26.7 us
  transfers between devices with their start and end apart: 10, of which 9 were waited for; matrix products, arithmetic and copies ran while one was open for 40% of the time, Pallas kernels for 0%

profile of v1, /device:TPU:0, one launch (start us, length us, event | category | flops | bytes accessed | tf_op | source)
XLA Modules:
  0.0 444.3 jit_solution(17135048042065690808)
XLA Ops:
  7.3 32.8 %all-gather.14.cloned.1.call-done = bf16[512,2048]{1,0:T(8,128)(2,1)} async-done(((bf16[512,256]{1,0:T(8,128)(2,1)}), bf16[512,2048]{1,0:T(8,128)(2,1)}) %all-gather.14.cloned.1.call-update) | async-done | bytes 2097168 | tf_op jit(solution)/shard_map/all_gather | solution.py:23
  40.1 3.3 broadcast_select_fusion.1
  43.4 2.8 broadcast_select_fusion
  47.1 24.4 %all-gather.30.cloned.1.call-done = bf16[1024,512]{1,0:T(8,128)(2,1)} async-done(((bf16[256,512]{1,0:T(8,128)(2,1)}), bf16[1024,512]{1,0:T(8,128)(2,1)}) %all-gather.30.cloned.1.call-update) | async-done | bytes 1048592 | tf_op jit(solution)/shard_map/all_gather | solution.py:10
  71.5 2.2 reduce_sum.37
  73.7 26.7 %all-gather.32.cloned.1.call-done = bf16[1024,512]{1,0:T(8,128)(2,1)} async-done(((bf16[256,512]{1,0:T(8,128)(2,1)}), bf16[1024,512]{1,0:T(8,128)(2,1)}) %all-gather.32.cloned.1.call-update) | async-done | bytes 1048592 | tf_op jit(solution)/shard_map/all_gather | solution.py:10
  100.5 2.1 reduce_sum.38
  104.2 25.1 %all-gather.28.cloned.1.call-done = bf16[256,2048]{1,0:T(8,128)(2,1)} async-done(((bf16[64,2048]{1,0:T(8,128)(2,1)}), bf16[256,2048]{1,0:T(8,128)(2,1)}) %all-gather.28.cloned.1.call-update) | async-done | bytes 1048592 | tf_op jit(solution)/shard_map/all_gather | solution.py:10
  129.3 1.4 reduce_sum.36
  130.7 27.5 %all-gather.16.cloned.1.call-done = bf16[2048,512]{1,0:T(8,128)(2,1)} async-done(((bf16[256,512]{1,0:T(8,128)(2,1)}), bf16[2048,512]{1,0:T(8,128)(2,1)}) %all-gather.16.cloned.1.call-update) | async-done | bytes 2097168 | tf_op jit(solution)/shard_map/all_gather | solution.py:47
  158.2 2.1 fusion.65
  160.3 27.5 %all-gather.18.cloned.1.call-done = bf16[2048,512]{1,0:T(8,128)(2,1)} async-done(((bf16[256,512]{1,0:T(8,128)(2,1)}), bf16[2048,512]{1,0:T(8,128)(2,1)}) %all-gather.18.cloned.1.call-update) | async-done | bytes 2097168 | tf_op jit(solution)/shard_map/all_gather | solution.py:48
  187.8 2.7 fusion.12
  190.8 26.7 %all-gather.22.cloned.1.call-done = bf16[2048,512]{1,0:T(8,128)(2,1)} async-done(((bf16[256,512]{1,0:T(8,128)(2,1)}), bf16[2048,512]{1,0:T(8,128)(2,1)}) %all-gather.22.cloned.1.call-update) | async-done | bytes 2097168 | tf_op jit(solution)/shard_map/all_gather | solution.py:33
  217.5 2.2 fusion.68
  219.7 27.5 %all-gather.24.cloned.1.call-done = bf16[2048,512]{1,0:T(8,128)(2,1)} async-done(((bf16[256,512]{1,0:T(8,128)(2,1)}), bf16[2048,512]{1,0:T(8,128)(2,1)}) %all-gather.24.cloned.1.call-update) | async-done | bytes 2097168 | tf_op jit(solution)/shard_map/all_gather | solution.py:34
  247.2 2.7 fusion.11
  249.9 6.0 %fusion.67 = f32[512,1024]{1,0:T(8,128)} fusion(bf16[2048,512]{1,0:T(8,128)(2,1)S(1)} %copy-done.7, bf16[1024,2048]{1,0:T(8,128)(2,1)} %param.4), kind=kOutput, calls=%fused_computation.112 | convolution fusion | flops 2147483648 | bytes 8388608 | tf_op jit(solution)/shard_map/dot_general | solution.py:38
  256.0 2.4 fusion.66
  258.4 3.7 multiply_multiply_fusion
  262.1 10.3 %all-gather.20.cloned.1.call-done = f32[512,512]{1,0:T(8,128)} async-done(((f32[64,512]{1,0:T(8,128)}), f32[512,512]{1,0:T(8,128)}) %all-gather.20.cloned.1.call-update) | async-done | bytes 1048592 | tf_op jit(solution)/shard_map/all_gather | solution.py:58
  272.5 1.6 copy.12
  275.3 11.9 %cholesky.104 = f32[128,128]{1,0:T(8,128)S(1)} custom-call(f32[128,128]{1,0:T(8,128)S(1)} %cholesky.266), custom_call_target="Cholesky" | custom-call | tf_op jit(solution)/shard_map/jit(cholesky)/cholesky | solution.py:59
  287.4 9.8 %custom-call.34 = f32[1,128,128]{1,2,0:T(8,128)S(1)} custom-call(f32[1,128,128]{2,1,0:T(8,128)S(1)} %get-tuple-element.32), custom_call_target="InvertDiagBlocksLowerTriangular" | custom-call | tf_op jit(solution)/shard_map/jit(cholesky)/cholesky | solution.py:59
  297.2 1.2 constant_dynamic-update-slice_fusion.3
  298.5 1.3 convolution_subtract_fusion.5
  299.7 11.7 %cholesky.217 = f32[128,128]{1,0:T(8,128)S(1)} custom-call(f32[128,128]{1,0:T(8,128)S(1)} %cholesky.270), custom_call_target="Cholesky" | custom-call | tf_op jit(solution)/shard_map/jit(cholesky)/cholesky | solution.py:59
  311.5 9.8 %custom-call.35 = f32[1,128,128]{1,2,0:T(8,128)S(1)} custom-call(f32[1,128,128]{2,1,0:T(8,128)S(1)} %get-tuple-element.29), custom_call_target="InvertDiagBlocksLowerTriangular" | custom-call | tf_op jit(solution)/shard_map/jit(cholesky)/cholesky | solution.py:59
  321.6 1.3 convolution_subtract_fusion.6
  322.9 12.1 %cholesky.238 = f32[128,128]{1,0:T(8,128)S(1)} custom-call(f32[128,128]{1,0:T(8,128)S(1)} %cholesky.275), custom_call_target="Cholesky" | custom-call | tf_op jit(solution)/shard_map/jit(cholesky)/cholesky | solution.py:59
  335.0 9.8 %custom-call.36 = f32[1,128,128]{1,2,0:T(8,128)S(1)} custom-call(f32[1,128,128]{2,1,0:T(8,128)S(1)} %get-tuple-element.26), custom_call_target="InvertDiagBlocksLowerTriangular" | custom-call | tf_op jit(solution)/shard_map/jit(cholesky)/cholesky | solution.py:59
  345.1 1.2 convolution_subtract_fusion.7
  346.3 11.7 %cholesky.255 = f32[128,128]{1,0:T(8,128)S(1)} custom-call(f32[128,128]{1,0:T(8,128)S(1)} %convolution_subtract_fusion.7), custom_call_target="Cholesky" | custom-call | tf_op jit(solution)/shard_map/jit(cholesky)/cholesky | solution.py:59
  362.7 10.6 %while.1 = (s32[]{:T(128)}, f32[512,512]{1,0:T(8,128)S(1)}, s32[4,2]{0,1:T(2,128)S(1)}, f32[4,128,128]{2,1,0:T(8,128)}, s32[]{:T(128)}) while((s32[]{:T(128)}, f32[512,512]{1,0:T(8,128)S(1)}, s32[4,2]{0,1:T(2,128)S(1)}, f32[4,128,128]{2,1,0:T(8,128)}, s32[]{:T(128)}) %tuple.29), condition=%wide.while_cond, body=%wide.while_body.sunk | while | flops 2 | bytes 132205 | solution.py:60
  363.3 2.0 bitcast_dynamic-update-slice_fusion.2
  366.0 2.0 bitcast_dynamic-update-slice_fusion.2
  368.6 2.0 bitcast_dynamic-update-slice_fusion.2
  371.3 2.0 bitcast_dynamic-update-slice_fusion.2
  373.3 40.3 %custom-call.37 = f32[4,128,128]{1,2,0:T(8,128)S(1)} custom-call(f32[4,128,128]{2,1,0:T(8,128)} %get-tuple-element.12), custom_call_target="InvertDiagBlocksLowerTriangular" | custom-call | tf_op jit(solution)/shard_map/jit(_solve_triangular)/triangular_solve | solution.py:60
  413.6 1.8 fusion.29
  415.4 1.6 convolution_subtract_fusion.1
  419.1 1.1 fusion.7
  420.2 1.4 fusion.56
  421.7 1.5 fusion.34
  423.1 1.3 convolution_subtract_fusion.3
  426.9 3.6 fusion.10
  430.5 3.8 fusion
  434.3 2.9 copy.14
  (88 shorter events, 14.6 us)
Async XLA Ops:
  6.5 33.5 %copy-start = (bf16[256,2048]{1,0:T(8,128)(2,1)S(1)}, bf16[256,2048]{1,0:T(8,128)(2,1)}, u32[]{:S(2)}) copy-start(bf16[256,2048]{1,0:T(8,128)(2,1)} %param.6) | copy-start | bytes 3145732
  6.5 33.5 %all-gather.14.cloned.1.call-start = ((), (), s32[]{:S(2)}) async-start(), calls=%async_computation | async-start | bytes 2359296 | tf_op jit(solution)/shard_map/all_gather | solution.py:23
  7.3 64.3 %all-gather.30.cloned.1.call-start = ((), (), s32[]{:S(2)}) async-start(), calls=%async_computation.8 | async-start | bytes 1310720 | tf_op jit(solution)/shard_map/all_gather | solution.py:10
  40.1 3.4 copy-start.12
  43.4 57.1 %all-gather.32.cloned.1.call-start = ((), (), s32[]{:S(2)}) async-start(), calls=%async_computation.9 | async-start | bytes 1310720 | tf_op jit(solution)/shard_map/all_gather | solution.py:10
  46.2 83.1 %all-gather.28.cloned.1.call-start = ((), (), s32[]{:S(2)}) async-start(), calls=%async_computation.7 | async-start | bytes 1310720 | tf_op jit(solution)/shard_map/all_gather | solution.py:10
  47.1 111.1 %all-gather.16.cloned.1.call-start = ((), (), s32[]{:S(2)}) async-start(), calls=%async_computation.1 | async-start | bytes 2359296 | tf_op jit(solution)/shard_map/all_gather | solution.py:47
  73.7 114.1 %all-gather.18.cloned.1.call-start = ((), (), s32[]{:S(2)}) async-start(), calls=%async_computation.2 | async-start | bytes 2359296 | tf_op jit(solution)/shard_map/all_gather | solution.py:48
  102.6 114.8 %all-gather.22.cloned.1.call-start = ((), (), s32[]{:S(2)}) async-start(), calls=%async_computation.4 | async-start | bytes 2359296 | tf_op jit(solution)/shard_map/all_gather | solution.py:33
  103.4 143.8 %all-gather.24.cloned.1.call-start = ((), (), s32[]{:S(2)}) async-start(), calls=%async_computation.5 | async-start | bytes 2359296 | tf_op jit(solution)/shard_map/all_gather | solution.py:34
  104.1 168.3 %all-gather.20.cloned.1.call-start = ((), (), s32[]{:S(2)}) async-start(), calls=%async_computation.3 | async-start | bytes 1179648 | tf_op jit(solution)/shard_map/all_gather | solution.py:58
  190.5 231.1 %all-gather.26.cloned.1.call-start = ((), (), s32[]{:S(2)}) async-start(), calls=%async_computation.6 | async-start | bytes 1179648 | tf_op jit(solution)/shard_map/all_gather | solution.py:44
  217.5 32.4 %copy-start.7 = (bf16[2048,512]{1,0:T(8,128)(2,1)S(1)}, bf16[2048,512]{1,0:T(8,128)(2,1)}, u32[]{:S(2)}) copy-start(bf16[2048,512]{1,0:T(8,128)(2,1)} %all-gather.22.cloned.1.call-done) | copy-start | bytes 6291460
  249.9 6.0 %copy-start.6 = (bf16[2048,512]{1,0:T(8,128)(2,1)S(1)}, bf16[2048,512]{1,0:T(8,128)(2,1)}, u32[]{:S(2)}) copy-start(bf16[2048,512]{1,0:T(8,128)(2,1)} %all-gather.16.cloned.1.call-done) | copy-start | bytes 6291460
  249.9 6.0 %copy-start.13 = (bf16[1024,2048]{1,0:T(8,128)(2,1)S(1)}, bf16[1024,2048]{1,0:T(8,128)(2,1)}, u32[]{:S(2)}) copy-start(bf16[1024,2048]{1,0:T(8,128)(2,1)} %param.4) | copy-start | bytes 12582916
  256.0 2.4 copy-start.4
  272.4 1.7 copy-start.1
  274.3 1.0 copy-start.2
  413.6 4.1 copy-start.5
  419.1 1.1 copy-start.8
  421.7 3.2 copy-start.10
  424.4 2.4 copy-start.9
  424.5 2.4 copy-start.11
  425.8 4.7 %copy-start.15 = (f32[512,1024]{1,0:T(8,128)S(1)}, f32[512,1024]{1,0:T(8,128)}, u32[]{:S(2)}) copy-start(f32[512,1024]{1,0:T(8,128)} %fusion.67) | copy-start | bytes 6291460
  426.9 3.7 copy-start.3
  426.9 3.7 copy-start.14
Sparse Core Ops, SparseCore 0:
  9.2 30.8 all-gather.13
  43.5 27.9 all-gather.29
  73.1 27.3 all-gather.31
  101.9 27.3 all-gather.27
  131.0 27.1 all-gather.15
  160.0 27.7 all-gather.17
  189.7 27.7 all-gather.21
  219.3 27.7 all-gather.23
  249.0 23.3 all-gather.19
  274.2 23.5 all-gather.25
